TPU v7x, 32 devices: a whole 2x2x4 slice. The times are simulated.
32 devices in a mesh: node: 8 (over z, x), rep: 4 (over y, core).
Axes of the slice: x: 2, y: 2, z: 4, core: 2. Of those that a mesh axis runs over, the one named last changes fastest.
Arguments:
- features: bfloat16 [8192, 512], P(('node', 'rep')), may hold values from -6 to 6
- weight: bfloat16 [512, 512], replicated, may hold values from -0.25 to 0.25
- cotangent: bfloat16 [8192, 512], P(('node', 'rep')), may hold values from -6 to 6
- tile_values: bfloat16 [8192, 128, 128], P(('node', 'rep')), may hold values from -0.125 to 0.125
- tile_row: int32 [8192], P(('node', 'rep')), may hold values from 0 to 7
- tile_col: int32 [8192], P(('node', 'rep')), may hold values from 0 to 15
- tile_count: int32 [32], P(('node', 'rep')), may hold values from 64 to 256, as said below
Outputs:
- activation: bfloat16 [8192, 512], P(('node', 'rep'))
- weight_grad: float32 [512, 512], replicated
- feature_grad: bfloat16 [8192, 512], P(('node', 'rep'))
Inputs may be any that keep to these rules, and one draw needn't show every extreme that they name: `tile_count`: slots of a device below its count hold tiles, the others are ignored; some device uses all 256 slots.
All inputs are finite; a program needn't handle non-finite values.
Results may differ from a plain program's by a relative error of at most 0.023.
Values may be sent and summed in bfloat16 or wider, within the bound.
A program may use at most 128 MiB of HBM per device.

v0:
```python
import math
import jax
import jax.numpy as jnp
from jax import lax
from jax.sharding import PartitionSpec as P

TB = 128


def smooth_gate(values):
    return jax.nn.gelu(values, approximate=True)


def apply_tiles(
    tile_values, tile_row, tile_col, tile_count, sources, target_shape, backward, window_start
):
    group_size = min(32, tile_row.shape[0])
    filled = tile_count[0]
    turns_needed = (filled + group_size - 1) // group_size
    window_blocks = target_shape[0]

    def one_turn(turn_index, totals):
        offset = turn_index * group_size
        values = lax.dynamic_slice_in_dim(tile_values, offset, group_size, 0)
        rows_here = lax.dynamic_slice_in_dim(tile_row, offset, group_size, 0)
        cols_here = lax.dynamic_slice_in_dim(tile_col, offset, group_size, 0)
        slot_mask = (offset + jnp.arange(group_size, dtype=jnp.int32) < filled).astype(jnp.float32)
        if backward:
            local_cols = cols_here - window_start
            inside = ((local_cols >= 0) & (local_cols < window_blocks)).astype(jnp.float32)
            placed = jnp.clip(local_cols, 0, window_blocks - 1)
            product = jnp.einsum(
                "tji,tjf->tif", values, sources[rows_here], preferred_element_type=jnp.float32
            )
            return totals.at[placed].add(product * (slot_mask * inside)[:, None, None])
        product = jnp.einsum(
            "tij,tjf->tif", values, sources[cols_here], preferred_element_type=jnp.float32
        )
        return totals.at[rows_here].add(product * slot_mask[:, None, None])

    return lax.fori_loop(0, turns_needed, one_turn, jnp.zeros(target_shape, jnp.float32))


def local(features, weight, cotangent, tile_values, tile_row, tile_col, tile_count):
    rows_quarter = features.shape[0]
    feature_width = features.shape[1]
    rep_count = lax.axis_size("rep")
    node_count = lax.axis_size("node")
    scale = 1.0 / math.sqrt(rows_quarter * rep_count * node_count)
    gathered = lax.all_gather(features, "node", axis=0, tiled=True)
    source_blocks = gathered.reshape(-1, TB, feature_width)
    block_count = rows_quarter * rep_count // TB
    partial_value = apply_tiles(
        tile_values,
        tile_row,
        tile_col,
        tile_count,
        source_blocks,
        (block_count, TB, feature_width),
        False,
        0,
    ).reshape(block_count * TB, feature_width)
    aggregate_all = lax.psum(partial_value, "rep").astype(jnp.bfloat16)
    cotangent_all = lax.all_gather(cotangent, "rep", axis=0, tiled=True)
    pre = jnp.dot(aggregate_all, weight, preferred_element_type=jnp.float32)
    activated, pullback = jax.vjp(smooth_gate, pre)
    grad_all = pullback(cotangent_all.astype(jnp.float32))[0].astype(jnp.bfloat16)
    full_grad = jnp.dot(grad_all, weight.T, preferred_element_type=jnp.float32).astype(jnp.bfloat16)
    offset = lax.axis_index("rep") * rows_quarter
    own_aggregate = lax.dynamic_slice_in_dim(aggregate_all, offset, rows_quarter, 0)
    own_grad = lax.dynamic_slice_in_dim(grad_all, offset, rows_quarter, 0)
    weight_term = jnp.dot(own_aggregate.T, own_grad, preferred_element_type=jnp.float32)
    output_rows = lax.dynamic_slice_in_dim(activated, offset, rows_quarter, 0).astype(jnp.bfloat16)
    weight_grad = lax.psum(weight_term, ("node", "rep")) * scale
    grad_blocks = full_grad.reshape(block_count, TB, feature_width)
    contributions = apply_tiles(
        tile_values, tile_row, tile_col, tile_count, grad_blocks, source_blocks.shape, True, 0
    )
    feature_grad = lax.psum_scatter(
        contributions.reshape(-1, feature_width).astype(jnp.bfloat16),
        "node",
        scatter_dimension=0,
        tiled=True,
    )
    return (output_rows, weight_grad, feature_grad)


def solution(mesh):
    in_specs = (
        P(("node", "rep"), None),
        P(),
        P(("node", "rep"), None),
        P(("node", "rep"), None, None),
        P(("node", "rep")),
        P(("node", "rep")),
        P(("node", "rep")),
    )
    out_specs = (P(("node", "rep"), None), P(), P(("node", "rep"), None))
    return jax.shard_map(local, mesh=mesh, in_specs=in_specs, out_specs=out_specs, check_vma=False)
```

profile of v0, /device:TPU:0, one launch (start us, length us, event | category | flops | bytes accessed | tf_op | source)
XLA Modules:
  0.0 611.5 jit_solution(17007301135434615890)
XLA Ops:
  7.2 0.7 all-gather.3.cloned.1.call-update
  8.0 0.7 all-gather.5.cloned.1.call-update
  9.4 52.6 %all-gather.3.cloned.1.call-done = bf16[2048,512]{1,0:T(8,128)(2,1)} async-done(((bf16[256,512]{1,0:T(8,128)(2,1)}), bf16[2048,512]{1,0:T(8,128)(2,1)}) %all-gather.3.cloned.1.call-update) | async-done | bytes 2097168 | tf_op jit(solution)/shard_map/all_gather | solution.py:50
  62.0 0.2 broadcast_in_dim.20
  62.3 95.9 %while.20 = (s32[]{:T(128)}, f32[8,128,512]{2,1,0:T(8,128)S(1)}, s32[]{:T(128)}, s32[256]{0:T(256)S(1)}, bf16[256,128,128]{2,1,0:T(8,128)(2,1)}, /*index=5*/s32[...) while((s32[]{:T(128)}, f32[8,128,512]{2,1,0:T(8,128)S(1)}, ...), condition=%wide.region_2.3_spmd, body=%wide.region_0.2_spmd.sunk | while | flops 541066560 | bytes 47191344 | solution.py:41
  62.3 0.7 compare_convert_fusion.3
  63.0 4.4 gather_fusion
  67.4 7.2 %broadcast_multiply_fusion.5 = f32[32,128,512]{2,1,0:T(8,128)} fusion(f32[32]{0:T(128)S(1)} %compare_convert_fusion.3, bf16[32,128,512]{2,1,0:T(8,128)(2,1)} %gather_fusion, bf16[256,128,128]{2,1,0:T(8,128)(2,1)} %get-tuple-element.274, s32[]{:T(128)S(6)} %select_n.44), kind=kOutput, calls=%fused_computation.4.clone.1 | convolution fusion | flops 538968064 | bytes 13631620 | tf_op jit(solution)/shard_map/while/body/tij,tjf->tif/dot_general | solution.py:36
  74.6 11.8 %scatter_fusion = f32[8,128,512]{2,1,0:T(8,128)S(1)} fusion(f32[8,128,512]{2,1,0:T(8,128)S(1)} %get-tuple-element.259, s32[32]{0:T(128)S(1)} %get-tuple-element.234, f32[32,128,512]{2,1,0:T(8,128)} %broadcast_multiply_fusion.5), kind=kCustom, calls=%fused_computation.2.clone.1 | custom fusion | flops 2097152 | bytes 25165952 | tf_op jit(solution)/shard_map/while/body/scatter-add | solution.py:39
  86.4 0.7 compare_convert_fusion.3
  87.2 4.4 gather_fusion
  91.5 7.0 %broadcast_multiply_fusion.5 = f32[32,128,512]{2,1,0:T(8,128)} fusion(f32[32]{0:T(128)S(1)} %compare_convert_fusion.3, bf16[32,128,512]{2,1,0:T(8,128)(2,1)} %gather_fusion, bf16[256,128,128]{2,1,0:T(8,128)(2,1)} %get-tuple-element.274, s32[]{:T(128)S(6)} %select_n.44), kind=kOutput, calls=%fused_computation.4.clone.1 | convolution fusion | flops 538968064 | bytes 13631620 | tf_op jit(solution)/shard_map/while/body/tij,tjf->tif/dot_general | solution.py:36
  98.5 11.8 %scatter_fusion = f32[8,128,512]{2,1,0:T(8,128)S(1)} fusion(f32[8,128,512]{2,1,0:T(8,128)S(1)} %get-tuple-element.259, s32[32]{0:T(128)S(1)} %get-tuple-element.234, f32[32,128,512]{2,1,0:T(8,128)} %broadcast_multiply_fusion.5), kind=kCustom, calls=%fused_computation.2.clone.1 | custom fusion | flops 2097152 | bytes 25165952 | tf_op jit(solution)/shard_map/while/body/scatter-add | solution.py:39
  110.3 0.7 compare_convert_fusion.3
  111.1 4.4 gather_fusion
  115.4 7.0 %broadcast_multiply_fusion.5 = f32[32,128,512]{2,1,0:T(8,128)} fusion(f32[32]{0:T(128)S(1)} %compare_convert_fusion.3, bf16[32,128,512]{2,1,0:T(8,128)(2,1)} %gather_fusion, bf16[256,128,128]{2,1,0:T(8,128)(2,1)} %get-tuple-element.274, s32[]{:T(128)S(6)} %select_n.44), kind=kOutput, calls=%fused_computation.4.clone.1 | convolution fusion | flops 538968064 | bytes 13631620 | tf_op jit(solution)/shard_map/while/body/tij,tjf->tif/dot_general | solution.py:36
  122.4 11.7 %scatter_fusion = f32[8,128,512]{2,1,0:T(8,128)S(1)} fusion(f32[8,128,512]{2,1,0:T(8,128)S(1)} %get-tuple-element.259, s32[32]{0:T(128)S(1)} %get-tuple-element.234, f32[32,128,512]{2,1,0:T(8,128)} %broadcast_multiply_fusion.5), kind=kCustom, calls=%fused_computation.2.clone.1 | custom fusion | flops 2097152 | bytes 25165952 | tf_op jit(solution)/shard_map/while/body/scatter-add | solution.py:39
  134.2 0.7 compare_convert_fusion.3
  134.9 4.4 gather_fusion
  139.3 7.0 %broadcast_multiply_fusion.5 = f32[32,128,512]{2,1,0:T(8,128)} fusion(f32[32]{0:T(128)S(1)} %compare_convert_fusion.3, bf16[32,128,512]{2,1,0:T(8,128)(2,1)} %gather_fusion, bf16[256,128,128]{2,1,0:T(8,128)(2,1)} %get-tuple-element.274, s32[]{:T(128)S(6)} %select_n.44), kind=kOutput, calls=%fused_computation.4.clone.1 | convolution fusion | flops 538968064 | bytes 13631620 | tf_op jit(solution)/shard_map/while/body/tij,tjf->tif/dot_general | solution.py:36
  146.3 11.8 %scatter_fusion = f32[8,128,512]{2,1,0:T(8,128)S(1)} fusion(f32[8,128,512]{2,1,0:T(8,128)S(1)} %get-tuple-element.259, s32[32]{0:T(128)S(1)} %get-tuple-element.234, f32[32,128,512]{2,1,0:T(8,128)} %broadcast_multiply_fusion.5), kind=kCustom, calls=%fused_computation.2.clone.1 | custom fusion | flops 2097152 | bytes 25165952 | tf_op jit(solution)/shard_map/while/body/scatter-add | solution.py:39
  158.1 87.7 %all-reduce.4 = bf16[1024,512]{1,0:T(8,128)(2,1)} all-reduce(f32[1024,512]{1,0:T(8,128)S(1)} %bitcast.16), channel_id=1, replica_groups=mesh['node'=8,'rep'=4] {'rep'}, use_global_device_ids=true, to_apply=%region_3.4 | all-reduce | flops 524288 | bytes 3145728 | tf_op jit(solution)/shard_map/psum | solution.py:63
  245.8 5.3 fusion.6
  251.2 0.7 convolution_convert_fusion
  251.9 2.3 fusion.15
  254.3 2.5 broadcast_in_dim.21
  256.8 117.3 %while.21 = (s32[]{:T(128)}, f32[16,128,512]{2,1,0:T(8,128)}, s32[]{:T(128)}, s32[256]{0:T(256)S(1)}, bf16[256,128,128]{2,1,0:T(8,128)(2,1)}, /*index=5*/s32[256...) while((s32[]{:T(128)}, f32[16,128,512]{2,1,0:T(8,128)}, ...), condition=%wide.region_7.8_spmd, body=%wide.region_5.7_spmd.sunk | while | flops 541066688 | bytes 47191480 | solution.py:41
  256.8 0.7 and_select_fusion.2
  257.6 2.8 gather_fusion.1
  260.3 7.3 %broadcast_multiply_fusion.6 = f32[32,128,512]{2,1,0:T(8,128)} fusion(f32[32]{0:T(128)S(1)} %and_select_fusion.2, bf16[32,128,512]{2,1,0:T(8,128)(2,1)} %gather_fusion.1, bf16[256,128,128]{2,1,0:T(8,128)(2,1)} %get-tuple-element.310, s32[]{:T(128)S(6)} %select_n.46), kind=kOutput, calls=%fused_computation.11.clone.1 | convolution fusion | flops 538968064 | bytes 13631620 | tf_op jit(solution)/shard_map/while/body/tji,tjf->tif/dot_general | solution.py:32
  267.6 18.4 %scatter_fusion.1 = f32[16,128,512]{2,1,0:T(8,128)} fusion(f32[16,128,512]{2,1,0:T(8,128)} %get-tuple-element.295, s32[32]{0:T(128)S(1)} %get-tuple-element.244, f32[32,128,512]{2,1,0:T(8,128)} %broadcast_multiply_fusion.6), kind=kCustom, calls=%fused_computation.3.clone.1 | custom fusion | flops 2097152 | bytes 25165952 | tf_op jit(solution)/shard_map/while/body/scatter-add | solution.py:35
  286.0 0.7 and_select_fusion.2
  286.8 2.8 gather_fusion.1
  289.5 7.3 %broadcast_multiply_fusion.6 = f32[32,128,512]{2,1,0:T(8,128)} fusion(f32[32]{0:T(128)S(1)} %and_select_fusion.2, bf16[32,128,512]{2,1,0:T(8,128)(2,1)} %gather_fusion.1, bf16[256,128,128]{2,1,0:T(8,128)(2,1)} %get-tuple-element.310, s32[]{:T(128)S(6)} %select_n.46), kind=kOutput, calls=%fused_computation.11.clone.1 | convolution fusion | flops 538968064 | bytes 13631620 | tf_op jit(solution)/shard_map/while/body/tji,tjf->tif/dot_general | solution.py:32
  296.8 18.7 %scatter_fusion.1 = f32[16,128,512]{2,1,0:T(8,128)} fusion(f32[16,128,512]{2,1,0:T(8,128)} %get-tuple-element.295, s32[32]{0:T(128)S(1)} %get-tuple-element.244, f32[32,128,512]{2,1,0:T(8,128)} %broadcast_multiply_fusion.6), kind=kCustom, calls=%fused_computation.3.clone.1 | custom fusion | flops 2097152 | bytes 25165952 | tf_op jit(solution)/shard_map/while/body/scatter-add | solution.py:35
  315.5 0.7 and_select_fusion.2
  316.3 2.8 gather_fusion.1
  319.0 7.3 %broadcast_multiply_fusion.6 = f32[32,128,512]{2,1,0:T(8,128)} fusion(f32[32]{0:T(128)S(1)} %and_select_fusion.2, bf16[32,128,512]{2,1,0:T(8,128)(2,1)} %gather_fusion.1, bf16[256,128,128]{2,1,0:T(8,128)(2,1)} %get-tuple-element.310, s32[]{:T(128)S(6)} %select_n.46), kind=kOutput, calls=%fused_computation.11.clone.1 | convolution fusion | flops 538968064 | bytes 13631620 | tf_op jit(solution)/shard_map/while/body/tji,tjf->tif/dot_general | solution.py:32
  326.3 18.3 %scatter_fusion.1 = f32[16,128,512]{2,1,0:T(8,128)} fusion(f32[16,128,512]{2,1,0:T(8,128)} %get-tuple-element.295, s32[32]{0:T(128)S(1)} %get-tuple-element.244, f32[32,128,512]{2,1,0:T(8,128)} %broadcast_multiply_fusion.6), kind=kCustom, calls=%fused_computation.3.clone.1 | custom fusion | flops 2097152 | bytes 25165952 | tf_op jit(solution)/shard_map/while/body/scatter-add | solution.py:35
  344.7 0.7 and_select_fusion.2
  345.5 2.8 gather_fusion.1
  348.2 7.3 %broadcast_multiply_fusion.6 = f32[32,128,512]{2,1,0:T(8,128)} fusion(f32[32]{0:T(128)S(1)} %and_select_fusion.2, bf16[32,128,512]{2,1,0:T(8,128)(2,1)} %gather_fusion.1, bf16[256,128,128]{2,1,0:T(8,128)(2,1)} %get-tuple-element.310, s32[]{:T(128)S(6)} %select_n.46), kind=kOutput, calls=%fused_computation.11.clone.1 | convolution fusion | flops 538968064 | bytes 13631620 | tf_op jit(solution)/shard_map/while/body/tji,tjf->tif/dot_general | solution.py:32
  355.5 18.5 %scatter_fusion.1 = f32[16,128,512]{2,1,0:T(8,128)} fusion(f32[16,128,512]{2,1,0:T(8,128)} %get-tuple-element.295, s32[32]{0:T(128)S(1)} %get-tuple-element.244, f32[32,128,512]{2,1,0:T(8,128)} %broadcast_multiply_fusion.6), kind=kCustom, calls=%fused_computation.3.clone.1 | custom fusion | flops 2097152 | bytes 25165952 | tf_op jit(solution)/shard_map/while/body/scatter-add | solution.py:35
  374.1 3.8 convert_element_type.37
  377.9 2.0 fusion.14
  379.9 49.0 %all-reduce.3.cloned.1.call-done = f32[512,512]{1,0:T(8,128)} async-done(((f32[512,512]{1,0:T(8,128)}), f32[512,512]{1,0:T(8,128)}) %all-reduce.3.cloned.1.call-update) | async-done | bytes 1048592 | tf_op jit(solution)/shard_map/psum | solution.py:74
  428.9 2.3 broadcast_multiply_fusion.2
  431.2 173.9 %reduce-scatter.2.cloned.1.call-done = bf16[256,512]{1,0:T(8,128)(2,1)} async-done(((bf16[2048,512]{1,0:T(8,128)(2,1)}), bf16[256,512]{1,0:T(8,128)(2,1)}) %reduce-scatter.2.cloned.1.call-update) | async-done | bytes 262160 | tf_op jit(solution)/shard_map/reduce_scatter | solution.py:79
  (29 shorter events, 0.9 us)
Async XLA Ops:
  7.2 238.7 %copy-start = (bf16[512,512]{1,0:T(8,128)(2,1)S(1)}, bf16[512,512]{1,0:T(8,128)(2,1)}, u32[]{:S(2)}) copy-start(bf16[512,512]{1,0:T(8,128)(2,1)} %param.12) | copy-start | bytes 1572868
  7.2 55.1 %copy-start.1 = (s32[256]{0:T(256)S(1)}, s32[256]{0:T(256)}, u32[]{:S(2)}) copy-start(s32[256]{0:T(256)} %param.16) | copy-start | bytes 3076
  7.2 55.1 %copy-start.2 = (s32[256]{0:T(256)S(1)}, s32[256]{0:T(256)}, u32[]{:S(2)}) copy-start(s32[256]{0:T(256)} %param.15) | copy-start | bytes 3076
  7.2 54.8 %all-gather.3.cloned.1.call-start = ((), (), s32[]{:S(2)}) async-start(), calls=%async_computation.1 | async-start | bytes 2359296 | tf_op jit(solution)/shard_map/all_gather | solution.py:50
  7.9 237.9 %all-gather.5.cloned.1.call-start = ((), (), s32[]{:S(2)}) async-start(), calls=%async_computation.2 | async-start | bytes 1310720 | tf_op jit(solution)/shard_map/all_gather | solution.py:64
  8.7 420.2 %all-reduce.3.cloned.1.call-start = ((), (), s32[]{:S(2)}) async-start(), calls=%async_computation.3 | async-start | bytes 2097152 | tf_op jit(solution)/shard_map/psum | solution.py:74
  254.2 350.8 %reduce-scatter.2.cloned.1.call-start = ((), (), s32[]{:S(2)}) async-start(), calls=%async_computation.4 | async-start | bytes 2359296 | tf_op jit(solution)/shard_map/reduce_scatter | solution.py:79
Sparse Core Ops, SparseCore 0:
  10.1 51.7 all-gather.2
  63.5 15.2 all-gather.4
  254.3 174.4 all-reduce.2
  432.8 172.1 reduce-scatter.1
where the time goes:
time: 614 us; the launch traced here: 612 us
  waiting for transfers between devices  277 us (45%)
  other arithmetic  135 us (22%)
  blocking collectives  87.7 us (14%)
  matrix products  65.7 us (11%)
  local copies, waits for them, and re-layouts  31.2 us (5%)
  between operations  14.5 us (2%)
    reduce_scatter x1, waiting for transfers between devices, local(): lax.psum_scatter(contributions.reshape(-1, feature_width).astype(jnp.bflo...  174 us
    psum x1, blocking collectives, local(): aggregate_all = lax.psum(partial_value, 'rep').astype(jnp.bfloat16)  87.7 us
    scatter-add x4, other arithmetic, one_turn(): return totals.at[placed].add(product * (slot_mask * inside)[:, None, None])  73.9 us
    all_gather x1, waiting for transfers between devices, local(): gathered = lax.all_gather(features, 'node', axis=0, tiled=True)  52.6 us
    psum x1, waiting for transfers between devices, local(): weight_grad = lax.psum(weight_term, ('node', 'rep')) * scale  49 us
    scatter-add x4, other arithmetic, one_turn(): return totals.at[rows_here].add(product * slot_mask[:, None, None])  47.1 us
    dot_general x4, matrix products, one_turn(): jnp.einsum('tji,tjf->tif', values, sources[rows_here], preferred_element_...  29.1 us
    dot_general x4, matrix products, one_turn(): jnp.einsum('tij,tjf->tif', values, sources[cols_here], preferred_element_...  28.2 us
  transfers between devices with their start and end apart: 4, of which 3 were waited for; matrix products, arithmetic and copies ran while one was open for 37% of the time, Pallas kernels for 0%

commit v1 on v0

--- a/solution.py
+++ b/solution.py
@@ -71,7 +71,12 @@
     own_grad = lax.dynamic_slice_in_dim(grad_all, offset, rows_quarter, 0)
     weight_term = jnp.dot(own_aggregate.T, own_grad, preferred_element_type=jnp.float32)
     output_rows = lax.dynamic_slice_in_dim(activated, offset, rows_quarter, 0).astype(jnp.bfloat16)
-    weight_grad = lax.psum(weight_term, ("node", "rep")) * scale
+
+    def map_the_windows(device_axis, a_name, own_rows):
+        f_now = lax.psum(lax.psum(own_rows, axis_name=a_name), axis_name=device_axis)
+        return f_now
+
+    weight_grad = map_the_windows("rep", "node", weight_term) * scale
     grad_blocks = full_grad.reshape(block_count, TB, feature_width)
     contributions = apply_tiles(
         tile_values, tile_row, tile_col, tile_count, grad_blocks, source_blocks.shape, True, 0

time: 614 us -> 689 us (1.12)
  waiting for transfers between devices: 277 us -> 352 us
    psum x1 -> x2, waiting for transfers between devices: 49 us -> 122 us  [the longest x1 122 us: map_the_windows(): lax.psum(own_rows, axis_name=a_name)]
  transfers between devices with their start and end apart: 4 -> 5, of which waited for: 3 -> 3; matrix products, arithmetic and copies ran while one was open for 37% -> 33% of each run, Pallas kernels for 0% -> 0%
where the time goes in v1:
time: 689 us; the launch traced here: 686 us
  waiting for transfers between devices  352 us (51%)
  other arithmetic  135 us (20%)
  blocking collectives  87.7 us (13%)
  matrix products  65.8 us (10%)
  local copies, waits for them, and re-layouts  31.3 us (5%)
  between operations  14.5 us (2%)
    reduce_scatter x1, waiting for transfers between devices, local(): lax.psum_scatter(contributions.reshape(-1, feature_width).astype(jnp.bflo...  176 us
    psum x1, waiting for transfers between devices, map_the_windows(): lax.psum(own_rows, axis_name=a_name)  122 us
    psum x1, blocking collectives, local(): aggregate_all = lax.psum(partial_value, 'rep').astype(jnp.bfloat16)  87.7 us
    scatter-add x4, other arithmetic, one_turn(): return totals.at[placed].add(product * (slot_mask * inside)[:, None, None])  73.7 us
    all_gather x1, waiting for transfers between devices, local(): gathered = lax.all_gather(features, 'node', axis=0, tiled=True)  52.6 us
    scatter-add x4, other arithmetic, one_turn(): return totals.at[rows_here].add(product * slot_mask[:, None, None])  47.1 us
    dot_general x4, matrix products, one_turn(): jnp.einsum('tji,tjf->tif', values, sources[rows_here], preferred_element_...  29.3 us
    dot_general x4, matrix products, one_turn(): jnp.einsum('tij,tjf->tif', values, sources[cols_here], preferred_element_...  28.2 us
  transfers between devices with their start and end apart: 5, of which 3 were waited for; matrix products, arithmetic and copies ran while one was open for 33% of the time, Pallas kernels for 0%

profile of v1, /device:TPU:0, one launch (start us, length us, event | category | flops | bytes accessed | tf_op | source)
XLA Modules:
  0.0 686.3 jit_solution(9550597787920115238)
XLA Ops:
  7.2 0.7 all-gather.3.cloned.1.call-update
  8.0 0.7 all-gather.5.cloned.1.call-update
  9.4 52.6 %all-gather.3.cloned.1.call-done = bf16[2048,512]{1,0:T(8,128)(2,1)} async-done(((bf16[256,512]{1,0:T(8,128)(2,1)}), bf16[2048,512]{1,0:T(8,128)(2,1)}) %all-gather.3.cloned.1.call-update) | async-done | bytes 2097168 | tf_op jit(solution)/shard_map/all_gather | solution.py:50
  62.0 0.2 broadcast_in_dim.20
  62.3 95.9 %while.20 = (s32[]{:T(128)}, f32[8,128,512]{2,1,0:T(8,128)S(1)}, s32[]{:T(128)}, s32[256]{0:T(256)S(1)}, bf16[256,128,128]{2,1,0:T(8,128)(2,1)}, /*index=5*/s32[...) while((s32[]{:T(128)}, f32[8,128,512]{2,1,0:T(8,128)S(1)}, ...), condition=%wide.region_2.3_spmd, body=%wide.region_0.2_spmd.sunk | while | flops 541066560 | bytes 47191344 | solution.py:41
  62.3 0.7 compare_convert_fusion.3
  63.0 4.4 gather_fusion
  67.4 7.2 %broadcast_multiply_fusion.5 = f32[32,128,512]{2,1,0:T(8,128)} fusion(f32[32]{0:T(128)S(1)} %compare_convert_fusion.3, bf16[32,128,512]{2,1,0:T(8,128)(2,1)} %gather_fusion, bf16[256,128,128]{2,1,0:T(8,128)(2,1)} %get-tuple-element.274, s32[]{:T(128)S(6)} %select_n.44), kind=kOutput, calls=%fused_computation.4.clone.1 | convolution fusion | flops 538968064 | bytes 13631620 | tf_op jit(solution)/shard_map/while/body/tij,tjf->tif/dot_general | solution.py:36
  74.6 11.8 %scatter_fusion = f32[8,128,512]{2,1,0:T(8,128)S(1)} fusion(f32[8,128,512]{2,1,0:T(8,128)S(1)} %get-tuple-element.259, s32[32]{0:T(128)S(1)} %get-tuple-element.234, f32[32,128,512]{2,1,0:T(8,128)} %broadcast_multiply_fusion.5), kind=kCustom, calls=%fused_computation.2.clone.1 | custom fusion | flops 2097152 | bytes 25165952 | tf_op jit(solution)/shard_map/while/body/scatter-add | solution.py:39
  86.4 0.7 compare_convert_fusion.3
  87.2 4.4 gather_fusion
  91.5 7.0 %broadcast_multiply_fusion.5 = f32[32,128,512]{2,1,0:T(8,128)} fusion(f32[32]{0:T(128)S(1)} %compare_convert_fusion.3, bf16[32,128,512]{2,1,0:T(8,128)(2,1)} %gather_fusion, bf16[256,128,128]{2,1,0:T(8,128)(2,1)} %get-tuple-element.274, s32[]{:T(128)S(6)} %select_n.44), kind=kOutput, calls=%fused_computation.4.clone.1 | convolution fusion | flops 538968064 | bytes 13631620 | tf_op jit(solution)/shard_map/while/body/tij,tjf->tif/dot_general | solution.py:36
  98.5 11.8 %scatter_fusion = f32[8,128,512]{2,1,0:T(8,128)S(1)} fusion(f32[8,128,512]{2,1,0:T(8,128)S(1)} %get-tuple-element.259, s32[32]{0:T(128)S(1)} %get-tuple-element.234, f32[32,128,512]{2,1,0:T(8,128)} %broadcast_multiply_fusion.5), kind=kCustom, calls=%fused_computation.2.clone.1 | custom fusion | flops 2097152 | bytes 25165952 | tf_op jit(solution)/shard_map/while/body/scatter-add | solution.py:39
  110.3 0.7 compare_convert_fusion.3
  111.1 4.4 gather_fusion
  115.4 7.0 %broadcast_multiply_fusion.5 = f32[32,128,512]{2,1,0:T(8,128)} fusion(f32[32]{0:T(128)S(1)} %compare_convert_fusion.3, bf16[32,128,512]{2,1,0:T(8,128)(2,1)} %gather_fusion, bf16[256,128,128]{2,1,0:T(8,128)(2,1)} %get-tuple-element.274, s32[]{:T(128)S(6)} %select_n.44), kind=kOutput, calls=%fused_computation.4.clone.1 | convolution fusion | flops 538968064 | bytes 13631620 | tf_op jit(solution)/shard_map/while/body/tij,tjf->tif/dot_general | solution.py:36
  122.4 11.7 %scatter_fusion = f32[8,128,512]{2,1,0:T(8,128)S(1)} fusion(f32[8,128,512]{2,1,0:T(8,128)S(1)} %get-tuple-element.259, s32[32]{0:T(128)S(1)} %get-tuple-element.234, f32[32,128,512]{2,1,0:T(8,128)} %broadcast_multiply_fusion.5), kind=kCustom, calls=%fused_computation.2.clone.1 | custom fusion | flops 2097152 | bytes 25165952 | tf_op jit(solution)/shard_map/while/body/scatter-add | solution.py:39
  134.2 0.7 compare_convert_fusion.3
  134.9 4.4 gather_fusion
  139.3 7.0 %broadcast_multiply_fusion.5 = f32[32,128,512]{2,1,0:T(8,128)} fusion(f32[32]{0:T(128)S(1)} %compare_convert_fusion.3, bf16[32,128,512]{2,1,0:T(8,128)(2,1)} %gather_fusion, bf16[256,128,128]{2,1,0:T(8,128)(2,1)} %get-tuple-element.274, s32[]{:T(128)S(6)} %select_n.44), kind=kOutput, calls=%fused_computation.4.clone.1 | convolution fusion | flops 538968064 | bytes 13631620 | tf_op jit(solution)/shard_map/while/body/tij,tjf->tif/dot_general | solution.py:36
  146.3 11.8 %scatter_fusion = f32[8,128,512]{2,1,0:T(8,128)S(1)} fusion(f32[8,128,512]{2,1,0:T(8,128)S(1)} %get-tuple-element.259, s32[32]{0:T(128)S(1)} %get-tuple-element.234, f32[32,128,512]{2,1,0:T(8,128)} %broadcast_multiply_fusion.5), kind=kCustom, calls=%fused_computation.2.clone.1 | custom fusion | flops 2097152 | bytes 25165952 | tf_op jit(solution)/shard_map/while/body/scatter-add | solution.py:39
  158.1 87.7 %all-reduce.7 = bf16[1024,512]{1,0:T(8,128)(2,1)} all-reduce(f32[1024,512]{1,0:T(8,128)S(1)} %bitcast.16), channel_id=1, replica_groups=mesh['node'=8,'rep'=4] {'rep'}, use_global_device_ids=true, to_apply=%region_3.4 | all-reduce | flops 524288 | bytes 3145728 | tf_op jit(solution)/shard_map/psum | solution.py:63
  245.8 5.3 fusion.6
  251.2 2.2 fusion.15
  253.5 0.7 convolution_convert_fusion
  254.2 121.5 %all-reduce.4.cloned.1.call-done = f32[512,512]{1,0:T(8,128)} async-done(((f32[512,512]{1,0:T(8,128)}), f32[512,512]{1,0:T(8,128)}) %all-reduce.4.cloned.1.call-update) | async-done | bytes 1048592 | tf_op jit(solution)/shard_map/psum | solution.py:76
  375.9 2.5 broadcast_in_dim.21
  378.3 117.3 %while.21 = (s32[]{:T(128)}, f32[16,128,512]{2,1,0:T(8,128)}, s32[]{:T(128)}, s32[256]{0:T(256)S(1)}, bf16[256,128,128]{2,1,0:T(8,128)(2,1)}, /*index=5*/s32[256...) while((s32[]{:T(128)}, f32[16,128,512]{2,1,0:T(8,128)}, ...), condition=%wide.region_8.9_spmd, body=%wide.region_6.8_spmd.sunk | while | flops 541066688 | bytes 47191480 | solution.py:41
  378.3 0.7 and_select_fusion.2
  379.1 2.8 gather_fusion.1
  381.9 7.5 %broadcast_multiply_fusion.6 = f32[32,128,512]{2,1,0:T(8,128)} fusion(f32[32]{0:T(128)S(1)} %and_select_fusion.2, bf16[32,128,512]{2,1,0:T(8,128)(2,1)} %gather_fusion.1, bf16[256,128,128]{2,1,0:T(8,128)(2,1)} %get-tuple-element.310, s32[]{:T(128)S(6)} %select_n.46), kind=kOutput, calls=%fused_computation.11.clone.1 | convolution fusion | flops 538968064 | bytes 13631620 | tf_op jit(solution)/shard_map/while/body/tji,tjf->tif/dot_general | solution.py:32
  389.4 18.6 %scatter_fusion.1 = f32[16,128,512]{2,1,0:T(8,128)} fusion(f32[16,128,512]{2,1,0:T(8,128)} %get-tuple-element.295, s32[32]{0:T(128)S(1)} %get-tuple-element.244, f32[32,128,512]{2,1,0:T(8,128)} %broadcast_multiply_fusion.6), kind=kCustom, calls=%fused_computation.3.clone.1 | custom fusion | flops 2097152 | bytes 25165952 | tf_op jit(solution)/shard_map/while/body/scatter-add | solution.py:35
  407.9 0.7 and_select_fusion.2
  408.7 2.8 gather_fusion.1
  411.5 7.3 %broadcast_multiply_fusion.6 = f32[32,128,512]{2,1,0:T(8,128)} fusion(f32[32]{0:T(128)S(1)} %and_select_fusion.2, bf16[32,128,512]{2,1,0:T(8,128)(2,1)} %gather_fusion.1, bf16[256,128,128]{2,1,0:T(8,128)(2,1)} %get-tuple-element.310, s32[]{:T(128)S(6)} %select_n.46), kind=kOutput, calls=%fused_computation.11.clone.1 | convolution fusion | flops 538968064 | bytes 13631620 | tf_op jit(solution)/shard_map/while/body/tji,tjf->tif/dot_general | solution.py:32
  418.8 18.5 %scatter_fusion.1 = f32[16,128,512]{2,1,0:T(8,128)} fusion(f32[16,128,512]{2,1,0:T(8,128)} %get-tuple-element.295, s32[32]{0:T(128)S(1)} %get-tuple-element.244, f32[32,128,512]{2,1,0:T(8,128)} %broadcast_multiply_fusion.6), kind=kCustom, calls=%fused_computation.3.clone.1 | custom fusion | flops 2097152 | bytes 25165952 | tf_op jit(solution)/shard_map/while/body/scatter-add | solution.py:35
  437.3 0.7 and_select_fusion.2
  438.1 2.8 gather_fusion.1
  440.9 7.3 %broadcast_multiply_fusion.6 = f32[32,128,512]{2,1,0:T(8,128)} fusion(f32[32]{0:T(128)S(1)} %and_select_fusion.2, bf16[32,128,512]{2,1,0:T(8,128)(2,1)} %gather_fusion.1, bf16[256,128,128]{2,1,0:T(8,128)(2,1)} %get-tuple-element.310, s32[]{:T(128)S(6)} %select_n.46), kind=kOutput, calls=%fused_computation.11.clone.1 | convolution fusion | flops 538968064 | bytes 13631620 | tf_op jit(solution)/shard_map/while/body/tji,tjf->tif/dot_general | solution.py:32
  448.2 18.2 %scatter_fusion.1 = f32[16,128,512]{2,1,0:T(8,128)} fusion(f32[16,128,512]{2,1,0:T(8,128)} %get-tuple-element.295, s32[32]{0:T(128)S(1)} %get-tuple-element.244, f32[32,128,512]{2,1,0:T(8,128)} %broadcast_multiply_fusion.6), kind=kCustom, calls=%fused_computation.3.clone.1 | custom fusion | flops 2097152 | bytes 25165952 | tf_op jit(solution)/shard_map/while/body/scatter-add | solution.py:35
  466.4 0.7 and_select_fusion.2
  467.2 2.8 gather_fusion.1
  469.9 7.3 %broadcast_multiply_fusion.6 = f32[32,128,512]{2,1,0:T(8,128)} fusion(f32[32]{0:T(128)S(1)} %and_select_fusion.2, bf16[32,128,512]{2,1,0:T(8,128)(2,1)} %gather_fusion.1, bf16[256,128,128]{2,1,0:T(8,128)(2,1)} %get-tuple-element.310, s32[]{:T(128)S(6)} %select_n.46), kind=kOutput, calls=%fused_computation.11.clone.1 | convolution fusion | flops 538968064 | bytes 13631620 | tf_op jit(solution)/shard_map/while/body/tji,tjf->tif/dot_general | solution.py:32
  477.2 18.5 %scatter_fusion.1 = f32[16,128,512]{2,1,0:T(8,128)} fusion(f32[16,128,512]{2,1,0:T(8,128)} %get-tuple-element.295, s32[32]{0:T(128)S(1)} %get-tuple-element.244, f32[32,128,512]{2,1,0:T(8,128)} %broadcast_multiply_fusion.6), kind=kCustom, calls=%fused_computation.3.clone.1 | custom fusion | flops 2097152 | bytes 25165952 | tf_op jit(solution)/shard_map/while/body/scatter-add | solution.py:35
  495.7 3.8 convert_element_type.37
  499.5 2.0 fusion.14
  501.5 2.3 broadcast_multiply_fusion.2
  503.8 176.0 %reduce-scatter.2.cloned.1.call-done = bf16[256,512]{1,0:T(8,128)(2,1)} async-done(((bf16[2048,512]{1,0:T(8,128)(2,1)}), bf16[256,512]{1,0:T(8,128)(2,1)}) %reduce-scatter.2.cloned.1.call-update) | async-done | bytes 262160 | tf_op jit(solution)/shard_map/reduce_scatter | solution.py:84
  (32 shorter events, 1.0 us)
Async XLA Ops:
  7.2 238.7 %copy-start = (bf16[512,512]{1,0:T(8,128)(2,1)S(1)}, bf16[512,512]{1,0:T(8,128)(2,1)}, u32[]{:S(2)}) copy-start(bf16[512,512]{1,0:T(8,128)(2,1)} %param.12) | copy-start | bytes 1572868
  7.2 55.1 %copy-start.1 = (s32[256]{0:T(256)S(1)}, s32[256]{0:T(256)}, u32[]{:S(2)}) copy-start(s32[256]{0:T(256)} %param.16) | copy-start | bytes 3076
  7.2 55.1 %copy-start.2 = (s32[256]{0:T(256)S(1)}, s32[256]{0:T(256)}, u32[]{:S(2)}) copy-start(s32[256]{0:T(256)} %param.15) | copy-start | bytes 3076
  7.2 54.8 %all-gather.3.cloned.1.call-start = ((), (), s32[]{:S(2)}) async-start(), calls=%async_computation.1 | async-start | bytes 2359296 | tf_op jit(solution)/shard_map/all_gather | solution.py:50
  7.9 237.9 %all-gather.5.cloned.1.call-start = ((), (), s32[]{:S(2)}) async-start(), calls=%async_computation.2 | async-start | bytes 1310720 | tf_op jit(solution)/shard_map/all_gather | solution.py:64
  8.7 367.1 %all-reduce.4.cloned.1.call-start = ((), (), s32[]{:S(2)}) async-start(), calls=%async_computation.3 | async-start | bytes 2097152 | tf_op jit(solution)/shard_map/psum | solution.py:76
  253.4 248.1 %all-reduce.6.cloned.1.call-start = ((), (), s32[]{:S(2)}) async-start(), calls=%async_computation.4 | async-start | bytes 2097152 | tf_op jit(solution)/shard_map/psum | solution.py:76
  375.8 304.0 %reduce-scatter.2.cloned.1.call-start = ((), (), s32[]{:S(2)}) async-start(), calls=%async_computation.5 | async-start | bytes 2359296 | tf_op jit(solution)/shard_map/reduce_scatter | solution.py:84
Sparse Core Ops, SparseCore 0:
  10.1 51.7 all-gather.2
  63.5 15.2 all-gather.4
  253.6 122.1 all-reduce.3
  378.0 35.8 all-reduce.5
  499.6 180.1 reduce-scatter.1
